TPU v7x, 128 devices: a whole 4x4x4 slice. The times are simulated.
128 devices in a mesh: req: 16 (over y, z), mlp: 8 (over x, core).
Axes of the slice: x: 4, y: 4, z: 4, core: 2. Of those that a mesh axis runs over, the one named last changes fastest.
Arguments:
- queries: bfloat16 [2048, 5120], P('req', 'mlp'), may hold values from -6 to 6
- leaf_keys: bfloat16 [2048, 1024], P('req', 'mlp'), may hold values from -6 to 6
- leaf_token_values: bfloat16 [2048, 1024], P('req', 'mlp'), may hold values from -6 to 6
- key_value_pages: bfloat16 [512, 64, 2, 1024], P('req', None, None, 'mlp'), may hold values from -6 to 6
- page_holder: int32 [16, 6, 4], replicated, may hold values from 0 to 15, as said below
- page_slot: int32 [16, 6, 4], replicated, may hold values from 0 to 31
- segment_ids: int32 [2048], P('req'), may hold values from 0 to 7, as said below
- req_parent: int32 [16, 8], P('req'), may hold values from 0 to 3
- mid_parent: int32 [16, 4], P('req'), may hold values from 0 to 1
- node_len: int32 [16, 6], P('req'), may hold values from 1 to 256
- residual: bfloat16 [2048, 5120], P('req'), may hold values from -6 to 6
- out_proj: bfloat16 [5120, 5120], P('mlp'), may hold values from -0.078125 to 0.078125
- norm_gain: float32 [5120], replicated, may hold values from 0.5 to 1.5
- gate_proj: bfloat16 [5120, 13824], P(None, ('req', 'mlp')), may hold values from -0.078125 to 0.078125
- up_proj: bfloat16 [5120, 13824], P(None, ('req', 'mlp')), may hold values from -0.078125 to 0.078125
- down_proj: bfloat16 [13824, 5120], P(('req', 'mlp')), may hold values from -0.0546875 to 0.0546875
- next_gain: float32 [5120], replicated, may hold values from 0.5 to 1.5
- qkv_proj: bfloat16 [5120, 7168], P(None, 'mlp'), may hold values from -0.078125 to 0.078125
- qkv_bias: float32 [7168], P('mlp'), may hold values from -3 to 3
Outputs:
- layer_out: bfloat16 [2048, 5120], P(('req', 'mlp'))
- qkv_out: bfloat16 [2048, 7168], P('req', 'mlp')
Inputs may be any that keep to these rules, and one draw needn't show every extreme that they name: `segment_ids`: within each block of 128 tokens of one group the ids never fall, start at 0, and every id 0 to 7 occurs. `page_holder`: in each row (one group's prefix pages) exactly half of the entries name the row's own group; the other entries name other groups, no group more than 1 times in a row, and some group exactly 1 times.
All inputs are finite; a program needn't handle non-finite values.
Results may differ from a plain program's by a relative error of at most 0.02.
Values may be sent and summed in bfloat16 or wider, within the bound.
A program may use at most 192 MiB of HBM per device.

v0:
```python
import math
import jax
import jax.numpy as jnp
from jax import lax
from jax.sharding import PartitionSpec as P

HEAD_SIZE = 128
QUERY_PER_KV = 5
REQ_DEV = 8
ROOT_DEV = 2
MID_DEV = 4
NODES_DEV = 6
NODE_MAX = 256
EPS = 1e-06


def rms_norm(stream, gain):
    values = stream.astype(jnp.float32)
    mean_sq = jnp.mean(values * values, axis=-1, keepdims=True)
    return (values * lax.rsqrt(mean_sq + EPS) * gain).astype(jnp.bfloat16)


def attend(
    queries,
    leaf_keys,
    leaf_token_values,
    prefix_keys,
    prefix_values,
    segments,
    parents,
    roots,
    lengths,
):
    tokens = queries.shape[0]
    heads_kv = leaf_keys.shape[1] // HEAD_SIZE
    query_rows = queries.reshape(tokens, heads_kv, QUERY_PER_KV, HEAD_SIZE)
    keys = jnp.concatenate(
        [
            prefix_keys.reshape(-1, heads_kv, HEAD_SIZE),
            leaf_keys.reshape(tokens, heads_kv, HEAD_SIZE),
        ],
        0,
    )
    values = jnp.concatenate(
        [
            prefix_values.reshape(-1, heads_kv, HEAD_SIZE),
            leaf_token_values.reshape(tokens, heads_kv, HEAD_SIZE),
        ],
        0,
    )
    middle = jnp.sum((segments[:, None] == jnp.arange(REQ_DEV)[None, :]) * parents[None, :], axis=1)
    root = jnp.sum((middle[:, None] == jnp.arange(MID_DEV)[None, :]) * roots[None, :], axis=1)
    node = jnp.arange(NODES_DEV * NODE_MAX) // NODE_MAX
    inside = (jnp.arange(NODE_MAX)[None, :] < lengths[:, None]).reshape(-1)
    prefix_mask = (
        (node[None, :] == root[:, None]) | (node[None, :] == ROOT_DEV + middle[:, None])
    ) & inside[None, :]
    place = jnp.arange(tokens)
    leaf_mask = (segments[None, :] == segments[:, None]) & (place[None, :] <= place[:, None])
    mask = jnp.concatenate([prefix_mask, leaf_mask], 1)
    score = jnp.einsum(
        "tkgd,skd->tkgs", query_rows, keys, preferred_element_type=jnp.float32
    ) / math.sqrt(HEAD_SIZE)
    score = jnp.where(mask[:, None, None, :], score, -1e30)
    top = jnp.max(score, axis=-1, keepdims=True)
    expo = jnp.where(mask[:, None, None, :], jnp.exp(score - top), 0.0)
    total = jnp.sum(expo, axis=-1, keepdims=True)
    weights = expo.astype(jnp.bfloat16)
    summed = jnp.einsum("tkgs,skd->tkgd", weights, values, preferred_element_type=jnp.float32)
    return (summed / total).astype(jnp.bfloat16).reshape(tokens, -1)


def fetch_prefix(key_value_pages, page_holder, page_slot):
    groups = lax.axis_size("req")
    myself = lax.axis_index("req")
    holders = page_holder.reshape(groups, -1)
    slots = page_slot.reshape(groups, -1)
    token_count = holders.shape[1]
    room = (token_count // 2 + groups - 2) // (groups - 1)
    earlier = jnp.arange(token_count)[None, :] < jnp.arange(token_count)[:, None]
    same = holders[:, :, None] == holders[:, None, :]
    rank = jnp.sum(same & earlier[None, :, :], axis=-1)
    asked = (holders == myself) & (jnp.arange(groups)[:, None] != myself)
    picked = asked[:, None, :] & (rank[:, None, :] == jnp.arange(room)[None, :, None])
    send_slot = jnp.sum(jnp.where(picked, slots[:, None, :], 0), axis=-1)
    outgoing = key_value_pages[send_slot]
    incoming = lax.all_to_all(outgoing, "req", split_axis=0, concat_axis=0, tiled=True)
    flat_in = incoming.reshape((groups * room,) + incoming.shape[2:])
    own_holders = lax.dynamic_index_in_dim(holders, myself, 0, keepdims=False)
    own_slots = lax.dynamic_index_in_dim(slots, myself, 0, keepdims=False)
    own_rank = lax.dynamic_index_in_dim(rank, myself, 0, keepdims=False)
    remote = flat_in[own_holders * room + jnp.minimum(own_rank, room - 1)]
    local = key_value_pages[own_slots]
    pages = jnp.where((own_holders == myself)[:, None, None, None], local, remote)
    return pages.reshape(NODES_DEV * NODE_MAX, 2, -1)


def body(
    queries,
    leaf_keys,
    leaf_token_values,
    key_value_pages,
    page_holder,
    page_slot,
    segment_ids,
    req_parent,
    mid_parent,
    node_len,
    residual,
    out_proj,
    norm_gain,
    gate_proj,
    up_proj,
    down_proj,
    next_gain,
    qkv_proj,
    qkv_bias,
):
    prefix = fetch_prefix(key_value_pages, page_holder, page_slot)
    attention = attend(
        queries,
        leaf_keys,
        leaf_token_values,
        prefix[:, 0],
        prefix[:, 1],
        segment_ids,
        req_parent[0],
        mid_parent[0],
        node_len[0],
    )
    projected = jnp.dot(attention, out_proj, preferred_element_type=jnp.float32)
    group_tokens = queries.shape[0]
    groups = lax.axis_size("req")
    members = lax.axis_size("mlp")
    rows_mlp = group_tokens // members
    first_row = lax.axis_index("mlp") * rows_mlp
    head_part = lax.psum_scatter(
        projected.astype(jnp.bfloat16), "mlp", scatter_dimension=0, tiled=True
    ).astype(jnp.float32)
    own_resid = lax.dynamic_slice_in_dim(residual, first_row, rows_mlp, 0)
    stream = (own_resid.astype(jnp.float32) + head_part).astype(jnp.bfloat16)
    normed = rms_norm(stream, norm_gain)
    piece = lax.all_gather(normed, ("req", "mlp"), axis=0, tiled=True)
    gate = jnp.dot(piece, gate_proj, preferred_element_type=jnp.float32)
    upper = jnp.dot(piece, up_proj, preferred_element_type=jnp.float32)
    hidden_all = (jax.nn.silu(gate) * upper).astype(jnp.bfloat16)
    blocks = hidden_all.reshape(groups, members, rows_mlp, -1)
    regrouped = lax.all_to_all(blocks, "mlp", split_axis=1, concat_axis=3, tiled=True)
    hidden = regrouped.reshape(groups * rows_mlp, -1)
    mixed_all = jnp.dot(
        hidden,
        lax.all_gather(down_proj, "mlp", axis=0, tiled=True),
        preferred_element_type=jnp.float32,
    )
    mixed = lax.psum_scatter(
        mixed_all.astype(jnp.bfloat16), "req", scatter_dimension=0, tiled=True
    ).astype(jnp.float32)
    layer_out = (stream.astype(jnp.float32) + mixed).astype(jnp.bfloat16)
    next_rows = rms_norm(layer_out, next_gain)
    next_normed = lax.all_gather(next_rows, "mlp", axis=0, tiled=True)
    qkv_out = (
        jnp.dot(next_normed, qkv_proj, preferred_element_type=jnp.float32) + qkv_bias
    ).astype(jnp.bfloat16)
    return (layer_out, qkv_out)


def solution(mesh):
    placed = (
        P("req", "mlp"),
        P("req", "mlp"),
        P("req", "mlp"),
        P("req", None, None, "mlp"),
        P(),
        P(),
        P("req"),
        P("req", None),
        P("req", None),
        P("req", None),
        P("req", None),
        P("mlp", None),
        P(),
        P(None, ("req", "mlp")),
        P(None, ("req", "mlp")),
        P(("req", "mlp"), None),
        P(),
        P(None, "mlp"),
        P("mlp"),
    )
    return jax.shard_map(
        body,
        mesh=mesh,
        in_specs=placed,
        out_specs=(P(("req", "mlp"), None), P("req", "mlp")),
        check_vma=False,
    )
```

profile of v0, /device:TPU:1, one launch (start us, length us, event | category | flops | bytes accessed | tf_op | source)
XLA Modules:
  0.0 356.3 jit_solution(15968638742785638937)
XLA Ops:
  7.2 0.9 copy.70
  8.1 0.4 convert_reduce_fusion
  8.6 0.1 copy.75
  8.7 0.8 select_reduce_fusion
  9.5 3.6 %gather_fusion.1 = bf16[16,64,2,128]{3,2,1,0:T(2,128)(2,1)} fusion(bf16[32,64,2,128]{3,2,1,0:T(2,128)(2,1)} %param.22, s32[1024]{0:T(1024)S(1)} %pad_clamp_fusion.1), kind=kCustom, calls=%fused_computation.1 | custom fusion | bytes 1048640 | tf_op jit(solution)/shard_map/gather | solution.py:86
  13.1 8.6 %all-to-all-start = ((bf16[16,1,64,2,128]{4,3,2,1,0:T(2,128)(2,1)}), bf16[16,1,64,2,128]{4,3,2,1,0:T(2,128)(2,1)S(1)}, u32[]{:S(2)}, u32[]{:S(2)}) async-start(bf16[16,1,64,2,128]{4,3,2,1,0:T(2,128)(2,1)} %bitcast.9), calls=%async_computation | async-start | bytes 1048576 | tf_op jit(solution)/shard_map/all_to_all | solution.py:87
  21.8 0.8 constant_dynamic-slice_fusion.1
  22.6 0.8 select_reduce_fusion.1
  23.4 0.7 select_reduce_fusion.2
  24.2 0.7 iota_compare_fusion.2
  24.9 1.7 or_and_fusion
  26.7 0.1 broadcast_in_dim.29
  26.8 3.4 gather_fusion
  30.1 0.2 copy.72
  30.4 0.8 copy.77
  31.2 0.1 fusion.30
  31.3 0.9 pad_add_fusion
  32.2 2.1 gather_fusion.2
  34.4 0.2 copy.76
  34.6 0.3 bitcast_select_fusion.1
  35.0 0.3 copy-done.4
  35.3 0.8 fusion
  36.1 1.0 fusion.1
  37.2 1.3 fusion.15
  38.4 1.0 slice-done.1
  39.5 2.3 convolution_convert_fusion.1
  41.9 31.3 %reduce-scatter.3.cloned.1.call-done = bf16[16,5120]{1,0:T(8,128)(2,1)} async-done(((bf16[128,5120]{1,0:T(8,128)(2,1)}), bf16[16,5120]{1,0:T(8,128)(2,1)}) %reduce-scatter.3.cloned.1.call-update) | async-done | bytes 163856 | tf_op jit(solution)/shard_map/reduce_scatter | solution.py:137
  73.2 1.2 fusion.26
  74.4 0.8 fusion.28
  75.2 0.2 all-gather.9.cloned.1.call-start
  75.4 0.5 all-gather.9.cloned.1.call-update
  75.9 90.1 %all-gather.5.cloned.1.call-done = bf16[2048,5120]{1,0:T(8,128)(2,1)} async-done(((bf16[16,5120]{1,0:T(8,128)(2,1)}), bf16[2048,5120]{1,0:T(8,128)(2,1)}) %all-gather.5.cloned.1.call-update) | async-done | bytes 20971536 | tf_op jit(solution)/shard_map/all_gather | solution.py:143
  166.1 13.8 %fusion.46 = f32[2048,108]{0,1:T(8,128)S(1)} fusion(bf16[2048,5120]{1,0:T(8,128)(2,1)} %all-gather.5.cloned.1.call-done, bf16[5120,108]{0,1:T(8,128)(2,1)S(1)} %copy-done), kind=kOutput, calls=%fused_computation.86 | convolution fusion | flops 2264924160 | bytes 22962176 | tf_op jit(solution)/shard_map/dot_general | solution.py:144
  179.9 0.6 copy-done.9
  180.5 6.8 %fusion.3 = bf16[2048,108]{0,1:T(8,128)(2,1)S(1)} fusion(bf16[2048,5120]{1,0:T(8,128)(2,1)S(1)} %copy-done.9, bf16[5120,108]{0,1:T(8,128)(2,1)S(1)} %copy-done.10, f32[2048,108]{0,1:T(8,128)S(1)} %fusion.46), kind=kOutput, calls=%fused_computation.11 | convolution fusion | flops 2266251264 | bytes 23404544 | tf_op jit(solution)/shard_map/dot_general | solution.py:145
  187.3 0.3 copy.81
  187.5 0.9 copy.82
  188.4 4.3 %all-to-all-start.1 = ((bf16[16,8,16,108]{3,2,0,1:T(8,128)(2,1)}), bf16[16,8,16,108]{3,2,0,1:T(8,128)(2,1)S(1)}, u32[]{:S(2)}, u32[]{:S(2)}) async-start(bf16[16,8,16,108]{3,2,0,1:T(8,128)(2,1)} %copy.82), calls=%async_computation.2 | async-start | bytes 1048576 | tf_op jit(solution)/shard_map/all_to_all | solution.py:148
  192.7 33.1 %all-gather.9.cloned.1.call-done = bf16[8,108,5120]{2,1,0:T(8,128)(2,1)} async-done(((bf16[1,108,5120]{2,1,0:T(8,128)(2,1)}), bf16[8,108,5120]{2,1,0:T(8,128)(2,1)}) %all-gather.9.cloned.1.call-update) | async-done | bytes 8847376 | tf_op jit(solution)/shard_map/all_gather | solution.py:152
  225.8 8.0 %reshape.279 = bf16[864,5120]{1,0:T(8,128)(2,1)} reshape(bf16[8,108,5120]{2,1,0:T(8,128)(2,1)} %all-gather.9.cloned.1.call-done) | data formatting | bytes 17694720
  233.8 0.3 copy.83
  234.1 0.4 reshape.253
  234.6 7.7 %convolution_convert_fusion = bf16[256,5120]{1,0:T(8,128)(2,1)} fusion(bf16[256,864]{1,0:T(8,128)(2,1)S(1)} %reshape.253, bf16[864,5120]{1,0:T(8,128)(2,1)} %reshape.279), kind=kOutput, calls=%fused_computation.3 | convolution fusion | flops 2266234880 | bytes 11911168 | tf_op jit(solution)/shard_map/dot_general | solution.py:150
  242.3 73.7 %reduce-scatter.5.cloned.1.call-done = bf16[16,5120]{1,0:T(8,128)(2,1)} async-done(((bf16[256,5120]{1,0:T(8,128)(2,1)}), bf16[16,5120]{1,0:T(8,128)(2,1)}) %reduce-scatter.5.cloned.1.call-update) | async-done | bytes 163856 | tf_op jit(solution)/shard_map/reduce_scatter | solution.py:155
  316.1 1.1 fusion.23
  317.2 0.8 fusion.25
  318.0 25.4 %all-gather.7.cloned.1.call-done = bf16[128,5120]{1,0:T(8,128)(2,1)} async-done(((bf16[16,5120]{1,0:T(8,128)(2,1)}), bf16[128,5120]{1,0:T(8,128)(2,1)}) %all-gather.7.cloned.1.call-update) | async-done | bytes 1310736 | tf_op jit(solution)/shard_map/all_gather | solution.py:160
  343.4 6.3 %fusion.8 = bf16[128,896]{1,0:T(8,128)(2,1)} fusion(bf16[128,5120]{1,0:T(8,128)(2,1)} %all-gather.7.cloned.1.call-done, bf16[5120,896]{1,0:T(8,128)(2,1)} %param.36, f32[896]{0:T(1024)S(1)} %copy-done.7), kind=kOutput, calls=%fused_computation.16 | convolution fusion | flops 1174634496 | bytes 10718720 | tf_op jit(solution)/shard_map/dot_general | solution.py:162
  (56 shorter events, 0.6 us)
Async XLA Ops:
  7.2 158.9 %copy-start = (bf16[5120,108]{0,1:T(8,128)(2,1)S(1)}, bf16[5120,108]{0,1:T(8,128)(2,1)}, u32[]{:S(2)}) copy-start(bf16[5120,108]{0,1:T(8,128)(2,1)} %param.32) | copy-start | bytes 3317764
  7.2 24.0 %copy-start.8 = (s32[128]{0:T(128)S(1)}, s32[128]{0:T(128)}, u32[]{:S(2)}) copy-start(s32[128]{0:T(128)} %param.25) | copy-start | bytes 1540
  7.2 23.2 %copy-start.3 = (bf16[128,640]{1,0:T(8,128)(2,1)S(1)}, bf16[128,640]{1,0:T(8,128)(2,1)}, u32[]{:S(2)}) copy-start(bf16[128,640]{1,0:T(8,128)(2,1)} %param.19) | copy-start | bytes 491524
  13.1 19.2 %all-to-all-start = ((bf16[16,1,64,2,128]{4,3,2,1,0:T(2,128)(2,1)}), bf16[16,1,64,2,128]{4,3,2,1,0:T(2,128)(2,1)S(1)}, u32[]{:S(2)}, u32[]{:S(2)}) async-start(bf16[16,1,64,2,128]{4,3,2,1,0:T(2,128)(2,1)} %bitcast.9), calls=%async_computation | async-start | bytes 1048576 | tf_op jit(solution)/shard_map/all_to_all | solution.py:87
  21.7 51.5 %reduce-scatter.3.cloned.1.call-start = ((), (), s32[]{:S(2)}) async-start(), calls=%async_computation.4 | async-start | bytes 1474560 | tf_op jit(solution)/shard_map/reduce_scatter | solution.py:137
  30.4 4.6 %copy-start.11 = (bf16[128,128]{1,0:T(8,128)(2,1)S(1)}, bf16[128,128]{1,0:T(8,128)(2,1)}, u32[]{:S(2)}) copy-start(bf16[128,128]{1,0:T(8,128)(2,1)} %param.20) | copy-start | bytes 98308
  34.4 0.9 copy-start.4
  35.3 1.9 copy-start.12
  36.1 2.4 slice-start
  37.1 2.3 slice-start.1
  39.5 34.9 %copy-start.5 = (f32[5120]{0:T(1024)S(1)}, f32[5120]{0:T(1024)}, u32[]{:S(2)}) copy-start(f32[5120]{0:T(1024)} %param.31) | copy-start | bytes 61444
  41.9 124.2 %all-gather.5.cloned.1.call-start = ((), (), s32[]{:S(2)}) async-start(), calls=%async_computation.5 | async-start | bytes 21135360 | tf_op jit(solution)/shard_map/all_gather | solution.py:143
  75.2 150.6 %all-gather.9.cloned.1.call-start = ((), (), s32[]{:S(2)}) async-start(), calls=%async_computation.8 | async-start | bytes 10321920 | tf_op jit(solution)/shard_map/all_gather | solution.py:152
  75.9 104.0 %copy-start.10 = (bf16[5120,108]{0,1:T(8,128)(2,1)S(1)}, bf16[5120,108]{0,1:T(8,128)(2,1)}, u32[]{:S(2)}) copy-start(bf16[5120,108]{0,1:T(8,128)(2,1)} %param.33) | copy-start | bytes 3317764
  166.1 14.4 %copy-start.9 = (bf16[2048,5120]{1,0:T(8,128)(2,1)S(1)}, bf16[2048,5120]{1,0:T(8,128)(2,1)}, u32[]{:S(2)}) copy-start(bf16[2048,5120]{1,0:T(8,128)(2,1)} %all-gather.5.cloned.1.call-done) | copy-start | bytes 62914564
  188.4 45.4 %all-to-all-start.1 = ((bf16[16,8,16,108]{3,2,0,1:T(8,128)(2,1)}), bf16[16,8,16,108]{3,2,0,1:T(8,128)(2,1)S(1)}, u32[]{:S(2)}, u32[]{:S(2)}) async-start(bf16[16,8,16,108]{3,2,0,1:T(8,128)(2,1)} %copy.82), calls=%async_computation.2 | async-start | bytes 1048576 | tf_op jit(solution)/shard_map/all_to_all | solution.py:148
  192.7 123.4 %reduce-scatter.5.cloned.1.call-start = ((), (), s32[]{:S(2)}) async-start(), calls=%async_computation.6 | async-start | bytes 2785280 | tf_op jit(solution)/shard_map/reduce_scatter | solution.py:155
  234.6 82.6 %copy-start.6 = (f32[5120]{0:T(1024)S(1)}, f32[5120]{0:T(1024)}, u32[]{:S(2)}) copy-start(f32[5120]{0:T(1024)} %param.35) | copy-start | bytes 61444
  234.6 108.8 %copy-start.7 = (f32[896]{0:T(1024)S(1)}, f32[896]{0:T(1024)}, u32[]{:S(2)}) copy-start(f32[896]{0:T(1024)} %param.37) | copy-start | bytes 10756
  242.3 101.1 %all-gather.7.cloned.1.call-start = ((), (), s32[]{:S(2)}) async-start(), calls=%async_computation.7 | async-start | bytes 1474560 | tf_op jit(solution)/shard_map/all_gather | solution.py:160
  317.1 32.6 %copy-start.2 = (bf16[16,5120]{1,0:T(8,128)(2,1)}, bf16[16,5120]{1,0:T(8,128)(2,1)S(1)}, u32[]{:S(2)}) copy-start(bf16[16,5120]{1,0:T(8,128)(2,1)S(1)} %get-tuple-element.3) | copy-start | bytes 491524
  343.4 6.3 %copy-start.1 = (bf16[5120,108]{0,1:T(8,128)(2,1)S(1)}, bf16[5120,108]{0,1:T(8,128)(2,1)}, u32[]{:S(2)}) copy-start(bf16[5120,108]{0,1:T(8,128)(2,1)} %param.32) | copy-start | bytes 3317764
Sparse Core Ops, SparseCore 0:
  42.0 31.1 reduce-scatter.2
  76.8 89.2 all-gather.4
  167.8 58.0 all-gather.8
  242.4 73.6 reduce-scatter.4
  318.2 25.1 all-gather.6
where the time goes:
time: 357 us; the launch traced here: 356 us
  waiting for transfers between devices  254 us (71%)
  matrix products  39 us (11%)
  local copies, waits for them, and re-layouts  24.3 us (7%)
  between operations  14.1 us (4%)
  starting transfers between devices  13.2 us (4%)
  other arithmetic  11.4 us (3%)
    all_gather x1, waiting for transfers between devices, body(): piece = lax.all_gather(normed, ('req', 'mlp'), axis=0, tiled=True)  90.1 us
    reduce_scatter x1, waiting for transfers between devices, body(): lax.psum_scatter(mixed_all.astype(jnp.bfloat16), 'req', scatter_dimension...  73.7 us
    all_gather x1, waiting for transfers between devices, body(): lax.all_gather(down_proj, 'mlp', axis=0, tiled=True)  33.1 us
    reduce_scatter x1, waiting for transfers between devices, body(): lax.psum_scatter(projected.astype(jnp.bfloat16), 'mlp', scatter_dimension...  31.3 us
    all_gather x1, waiting for transfers between devices, body(): next_normed = lax.all_gather(next_rows, 'mlp', axis=0, tiled=True)  25.4 us
    dot_general x1, matrix products, body(): gate = jnp.dot(piece, gate_proj, preferred_element_type=jnp.float32)  13.8 us
    unnamed x33, local copies, waits for them, and re-layouts  10.9 us
    all_to_all x1, starting transfers between devices, fetch_prefix(): lax.all_to_all(outgoing, 'req', split_axis=0, concat_axis=0, tiled=True)  8.6 us
  transfers between devices with their start and end apart: 7, of which 5 were waited for; matrix products, arithmetic and copies ran while one was open for 11% of the time, Pallas kernels for 0%

commit v1 on v0

--- a/solution.py
+++ b/solution.py
@@ -140,7 +140,8 @@
     own_resid = lax.dynamic_slice_in_dim(residual, first_row, rows_mlp, 0)
     stream = (own_resid.astype(jnp.float32) + head_part).astype(jnp.bfloat16)
     normed = rms_norm(stream, norm_gain)
-    piece = lax.all_gather(normed, ("req", "mlp"), axis=0, tiled=True)
+    sent = jnp.stack([normed] * lax.axis_size(("req", "mlp")))
+    piece = jnp.concatenate(lax.all_to_all(sent, ("req", "mlp"), 0, 0), axis=0)
     gate = jnp.dot(piece, gate_proj, preferred_element_type=jnp.float32)
     upper = jnp.dot(piece, up_proj, preferred_element_type=jnp.float32)
     hidden_all = (jax.nn.silu(gate) * upper).astype(jnp.bfloat16)

time: 357 us -> 588 us (1.65)
  waiting for transfers between devices: 254 us -> 452 us
  starting transfers between devices: 13.2 us -> 36.1 us
  local copies, waits for them, and re-layouts: 24.3 us -> 31.2 us
    all_to_all x0 -> x1, waiting for transfers between devices: none -> 319 us  [body(): piece = jnp.concatenate(lax.all_to_all(sent, ('req', 'mlp'), 0, 0), axis=0)]
    all_gather x1 -> x0, waiting for transfers between devices: 90.1 us -> none  [body(): piece = lax.all_gather(normed, ('req', 'mlp'), axis=0, tiled=True)]
    all_gather x1, waiting for transfers between devices: 33.1 us -> 0.01 us  [body(): lax.all_gather(down_proj, 'mlp', axis=0, tiled=True)]
    all_to_all x1, starting transfers between devices: 4.27 us -> 16.8 us  [body(): lax.all_to_all(blocks, 'mlp', split_axis=1, concat_axis=3, tiled=True)]
    all_to_all x0 -> x1, starting transfers between devices: none -> 10.3 us  [body(): piece = jnp.concatenate(lax.all_to_all(sent, ('req', 'mlp'), 0, 0), axis=0)]
    another operation x0 -> x1, local copies, waits for them, and re-layouts: none -> 7.56 us  [body(): sent = jnp.stack([normed] * lax.axis_size(('req', 'mlp')))]
    dot_general x1, matrix products: 6.76 us -> 13.8 us  [body(): upper = jnp.dot(piece, up_proj, preferred_element_type=jnp.float32)]
  transfers between devices with their start and end apart: 7 -> 7, of which waited for: 5 -> 5; matrix products, arithmetic and copies ran while one was open for 11% -> 8% of each run, Pallas kernels for 0% -> 0%
where the time goes in v1:
time: 588 us; the launch traced here: 587 us
  waiting for transfers between devices  452 us (77%)
  matrix products  43.2 us (7%)
  starting transfers between devices  36.1 us (6%)
  local copies, waits for them, and re-layouts  31.2 us (5%)
  between operations  14.1 us (2%)
  other arithmetic  10.8 us (2%)
    all_to_all x1, waiting for transfers between devices, body(): piece = jnp.concatenate(lax.all_to_all(sent, ('req', 'mlp'), 0, 0), axis=0)  319 us
    reduce_scatter x1, waiting for transfers between devices, body(): lax.psum_scatter(mixed_all.astype(jnp.bfloat16), 'req', scatter_dimension...  73.7 us
    reduce_scatter x1, waiting for transfers between devices, body(): lax.psum_scatter(projected.astype(jnp.bfloat16), 'mlp', scatter_dimension...  31.4 us
    all_gather x1, waiting for transfers between devices, body(): next_normed = lax.all_gather(next_rows, 'mlp', axis=0, tiled=True)  25.5 us
    all_to_all x1, starting transfers between devices, body(): lax.all_to_all(blocks, 'mlp', split_axis=1, concat_axis=3, tiled=True)  16.8 us
    dot_general x1, matrix products, body(): upper = jnp.dot(piece, up_proj, preferred_element_type=jnp.float32)  13.8 us
  transfers between devices with their start and end apart: 7, of which 5 were waited for; matrix products, arithmetic and copies ran while one was open for 8% of the time, Pallas kernels for 0%

profile of v1, /device:TPU:1, one launch (start us, length us, event | category | flops | bytes accessed | tf_op | source)
XLA Modules:
  0.0 587.2 jit_solution(14922693148626995798)
XLA Ops:
  7.2 0.9 copy.70
  8.1 0.4 convert_reduce_fusion
  8.6 0.1 copy.75
  8.7 0.8 select_reduce_fusion
  9.5 3.6 gather_fusion.1
  13.1 8.6 %all-to-all-start = ((bf16[16,1,64,2,128]{4,3,2,1,0:T(2,128)(2,1)}), bf16[16,1,64,2,128]{4,3,2,1,0:T(2,128)(2,1)S(1)}, u32[]{:S(2)}, u32[]{:S(2)}) async-start(bf16[16,1,64,2,128]{4,3,2,1,0:T(2,128)(2,1)} %bitcast.9), calls=%async_computation | async-start | bytes 1048576 | tf_op jit(solution)/shard_map/all_to_all | solution.py:87
  21.8 0.8 constant_dynamic-slice_fusion.1
  22.7 0.8 select_reduce_fusion.1
  23.4 0.7 select_reduce_fusion.2
  24.2 0.7 iota_compare_fusion.2
  24.9 1.7 or_and_fusion
  26.7 0.1 broadcast_in_dim.29
  26.8 3.4 gather_fusion
  30.2 0.2 copy.72
  30.4 0.8 copy.77
  31.3 0.9 pad_add_fusion
  32.2 2.1 gather_fusion.2
  34.4 0.2 copy.76
  34.6 0.3 bitcast_select_fusion.1
  35.0 0.3 copy-done.4
  35.3 0.8 fusion
  36.1 1.0 fusion.1
  37.2 1.3 fusion.15
  38.5 1.0 slice-done.1
  39.5 2.3 convolution_convert_fusion.1
  41.8 31.4 %reduce-scatter.3.cloned.1.call-done = bf16[16,5120]{1,0:T(8,128)(2,1)} async-done(((bf16[128,5120]{1,0:T(8,128)(2,1)}), bf16[16,5120]{1,0:T(8,128)(2,1)}) %reduce-scatter.3.cloned.1.call-update) | async-done | bytes 163856 | tf_op jit(solution)/shard_map/reduce_scatter | solution.py:137
  73.3 1.2 fusion.26
  74.4 0.1 fusion.28
  74.5 7.6 %stack.2 = bf16[128,16,5120]{2,1,0:T(8,128)(2,1)} broadcast(bf16[16,5120]{1,0:T(8,128)(2,1)S(1)} %fusion.28), dimensions={1,2} | broadcast | bytes 21135360 | tf_op jit(solution)/shard_map/stack | solution.py:143
  82.1 10.3 %all-to-all-start.1 = ((bf16[128,16,5120]{2,1,0:T(8,128)(2,1)}), bf16[128,16,5120]{2,1,0:T(8,128)(2,1)}, u32[]{:S(2)}, u32[]{:S(2)}) async-start(bf16[128,16,5120]{2,1,0:T(8,128)(2,1)} %stack.2), calls=%async_computation.2 | async-start | bytes 41943040 | tf_op jit(solution)/shard_map/all_to_all | solution.py:144
  92.4 0.2 all-gather.6.cloned.1.call-start
  92.7 0.5 all-gather.6.cloned.1.call-update
  93.2 319.1 %all-to-all-done.1 = bf16[128,16,5120]{2,1,0:T(8,128)(2,1)} async-done(((bf16[128,16,5120]{2,1,0:T(8,128)(2,1)}), bf16[128,16,5120]{2,1,0:T(8,128)(2,1)}, u32[]{:S(2)}, u32[]{:S(2)}) %all-to-all-start.1) | async-done | bytes 20971552 | tf_op jit(solution)/shard_map/all_to_all | solution.py:144
  412.3 11.1 %fusion.46 = f32[2048,108]{0,1:T(8,128)S(1)} fusion(bf16[2048,5120]{1,0:T(8,128)(2,1)} %bitcast.30, bf16[5120,108]{0,1:T(8,128)(2,1)S(1)} %copy-done), kind=kOutput, calls=%fused_computation.86 | convolution fusion | flops 2264924160 | bytes 22962176 | tf_op jit(solution)/shard_map/dot_general | solution.py:145
  423.4 13.8 %fusion.3 = bf16[2048,108]{0,1:T(8,128)(2,1)S(1)} fusion(bf16[2048,5120]{1,0:T(8,128)(2,1)} %bitcast.30, bf16[5120,108]{0,1:T(8,128)(2,1)S(1)} %copy-done.9, f32[2048,108]{0,1:T(8,128)S(1)} %fusion.46), kind=kOutput, calls=%fused_computation.11 | convolution fusion | flops 2266251264 | bytes 23404544 | tf_op jit(solution)/shard_map/dot_general | solution.py:146
  437.2 0.3 copy.81
  437.5 0.9 copy.82
  438.3 16.8 %all-to-all-start.2 = ((bf16[16,8,16,108]{3,2,0,1:T(8,128)(2,1)}), bf16[16,8,16,108]{3,2,0,1:T(8,128)(2,1)S(1)}, u32[]{:S(2)}, u32[]{:S(2)}) async-start(bf16[16,8,16,108]{3,2,0,1:T(8,128)(2,1)} %copy.82), calls=%async_computation.3 | async-start | bytes 1048576 | tf_op jit(solution)/shard_map/all_to_all | solution.py:149
  455.2 8.0 %reshape.285 = bf16[864,5120]{1,0:T(8,128)(2,1)} reshape(bf16[8,108,5120]{2,1,0:T(8,128)(2,1)} %all-gather.6.cloned.1.call-done) | data formatting | bytes 17694720
  463.1 1.5 all-to-all-done.2
  464.7 0.3 copy.83
  465.0 0.4 reshape.259
  465.5 7.7 %convolution_convert_fusion = bf16[256,5120]{1,0:T(8,128)(2,1)} fusion(bf16[256,864]{1,0:T(8,128)(2,1)S(1)} %reshape.259, bf16[864,5120]{1,0:T(8,128)(2,1)} %reshape.285), kind=kOutput, calls=%fused_computation.3 | convolution fusion | flops 2266234880 | bytes 11911168 | tf_op jit(solution)/shard_map/dot_general | solution.py:151
  473.2 73.7 %reduce-scatter.5.cloned.1.call-done = bf16[16,5120]{1,0:T(8,128)(2,1)} async-done(((bf16[256,5120]{1,0:T(8,128)(2,1)}), bf16[16,5120]{1,0:T(8,128)(2,1)}) %reduce-scatter.5.cloned.1.call-update) | async-done | bytes 163856 | tf_op jit(solution)/shard_map/reduce_scatter | solution.py:156
  546.9 1.1 fusion.23
  548.1 0.8 fusion.25
  548.9 25.5 %all-gather.4.cloned.1.call-done = bf16[128,5120]{1,0:T(8,128)(2,1)} async-done(((bf16[16,5120]{1,0:T(8,128)(2,1)}), bf16[128,5120]{1,0:T(8,128)(2,1)}) %all-gather.4.cloned.1.call-update) | async-done | bytes 1310736 | tf_op jit(solution)/shard_map/all_gather | solution.py:161
  574.3 6.3 %fusion.8 = bf16[128,896]{1,0:T(8,128)(2,1)} fusion(bf16[128,5120]{1,0:T(8,128)(2,1)} %all-gather.4.cloned.1.call-done, bf16[5120,896]{1,0:T(8,128)(2,1)} %param.36, f32[896]{0:T(1024)S(1)} %copy-done.7), kind=kOutput, calls=%fused_computation.16 | convolution fusion | flops 1174634496 | bytes 10718720 | tf_op jit(solution)/shard_map/dot_general | solution.py:163
  (54 shorter events, 0.6 us)
Async XLA Ops:
  7.2 405.1 %copy-start = (bf16[5120,108]{0,1:T(8,128)(2,1)S(1)}, bf16[5120,108]{0,1:T(8,128)(2,1)}, u32[]{:S(2)}) copy-start(bf16[5120,108]{0,1:T(8,128)(2,1)} %param.32) | copy-start | bytes 3317764
  7.2 24.0 %copy-start.8 = (s32[128]{0:T(128)S(1)}, s32[128]{0:T(128)}, u32[]{:S(2)}) copy-start(s32[128]{0:T(128)} %param.25) | copy-start | bytes 1540
  7.2 23.2 %copy-start.3 = (bf16[128,640]{1,0:T(8,128)(2,1)S(1)}, bf16[128,640]{1,0:T(8,128)(2,1)}, u32[]{:S(2)}) copy-start(bf16[128,640]{1,0:T(8,128)(2,1)} %param.19) | copy-start | bytes 491524
  13.1 19.2 %all-to-all-start = ((bf16[16,1,64,2,128]{4,3,2,1,0:T(2,128)(2,1)}), bf16[16,1,64,2,128]{4,3,2,1,0:T(2,128)(2,1)S(1)}, u32[]{:S(2)}, u32[]{:S(2)}) async-start(bf16[16,1,64,2,128]{4,3,2,1,0:T(2,128)(2,1)} %bitcast.9), calls=%async_computation | async-start | bytes 1048576 | tf_op jit(solution)/shard_map/all_to_all | solution.py:87
  21.7 51.6 %reduce-scatter.3.cloned.1.call-start = ((), (), s32[]{:S(2)}) async-start(), calls=%async_computation.5 | async-start | bytes 1474560 | tf_op jit(solution)/shard_map/reduce_scatter | solution.py:137
  30.4 4.6 copy-start.10
  34.4 0.9 copy-start.4
  35.3 1.9 copy-start.11
  36.1 2.4 slice-start
  37.2 2.3 slice-start.1
  39.5 34.9 %copy-start.5 = (f32[5120]{0:T(1024)S(1)}, f32[5120]{0:T(1024)}, u32[]{:S(2)}) copy-start(f32[5120]{0:T(1024)} %param.31) | copy-start | bytes 61444
  82.1 330.2 %all-to-all-start.1 = ((bf16[128,16,5120]{2,1,0:T(8,128)(2,1)}), bf16[128,16,5120]{2,1,0:T(8,128)(2,1)}, u32[]{:S(2)}, u32[]{:S(2)}) async-start(bf16[128,16,5120]{2,1,0:T(8,128)(2,1)} %stack.2), calls=%async_computation.2 | async-start | bytes 41943040 | tf_op jit(solution)/shard_map/all_to_all | solution.py:144
  92.4 362.7 %all-gather.6.cloned.1.call-start = ((), (), s32[]{:S(2)}) async-start(), calls=%async_computation.8 | async-start | bytes 10321920 | tf_op jit(solution)/shard_map/all_gather | solution.py:153
  412.3 11.1 %copy-start.9 = (bf16[5120,108]{0,1:T(8,128)(2,1)S(1)}, bf16[5120,108]{0,1:T(8,128)(2,1)}, u32[]{:S(2)}) copy-start(bf16[5120,108]{0,1:T(8,128)(2,1)} %param.33) | copy-start | bytes 3317764
  438.3 26.3 %all-to-all-start.2 = ((bf16[16,8,16,108]{3,2,0,1:T(8,128)(2,1)}), bf16[16,8,16,108]{3,2,0,1:T(8,128)(2,1)S(1)}, u32[]{:S(2)}, u32[]{:S(2)}) async-start(bf16[16,8,16,108]{3,2,0,1:T(8,128)(2,1)} %copy.82), calls=%async_computation.3 | async-start | bytes 1048576 | tf_op jit(solution)/shard_map/all_to_all | solution.py:149
  455.2 91.8 %reduce-scatter.5.cloned.1.call-start = ((), (), s32[]{:S(2)}) async-start(), calls=%async_computation.6 | async-start | bytes 2785280 | tf_op jit(solution)/shard_map/reduce_scatter | solution.py:156
  465.4 82.6 %copy-start.6 = (f32[5120]{0:T(1024)S(1)}, f32[5120]{0:T(1024)}, u32[]{:S(2)}) copy-start(f32[5120]{0:T(1024)} %param.35) | copy-start | bytes 61444
  465.5 108.9 %copy-start.7 = (f32[896]{0:T(1024)S(1)}, f32[896]{0:T(1024)}, u32[]{:S(2)}) copy-start(f32[896]{0:T(1024)} %param.37) | copy-start | bytes 10756
  473.2 101.1 %all-gather.4.cloned.1.call-start = ((), (), s32[]{:S(2)}) async-start(), calls=%async_computation.7 | async-start | bytes 1474560 | tf_op jit(solution)/shard_map/all_gather | solution.py:161
  548.0 32.6 %copy-start.2 = (bf16[16,5120]{1,0:T(8,128)(2,1)}, bf16[16,5120]{1,0:T(8,128)(2,1)S(1)}, u32[]{:S(2)}) copy-start(bf16[16,5120]{1,0:T(8,128)(2,1)S(1)} %get-tuple-element.3) | copy-start | bytes 491524
  574.3 6.3 %copy-start.1 = (bf16[5120,108]{0,1:T(8,128)(2,1)S(1)}, bf16[5120,108]{0,1:T(8,128)(2,1)}, u32[]{:S(2)}) copy-start(bf16[5120,108]{0,1:T(8,128)(2,1)} %param.32) | copy-start | bytes 3317764
Sparse Core Ops, SparseCore 0:
  42.0 31.2 reduce-scatter.2
  95.0 123.4 all-gather.5
  473.3 73.6 reduce-scatter.4
  549.1 25.2 all-gather.3
